TPU v7x, 32 devices: a whole 2x2x4 slice. The times are simulated.
32 devices in a mesh: sx: 8 (over z, y), sy: 4 (over x, core).
Axes of the slice: x: 2, y: 2, z: 4, core: 2. Of those that a mesh axis runs over, the one named last changes fastest.
Arguments:
- schur: bfloat16 [8, 4096, 4096], P('sx', 'sy'), as said below
- precond: bfloat16 [8, 4096, 4096], P('sx', 'sy'), as said below
- right_side: float32 [8, 32, 2048], P('sx', None, 'sy')
- matching: int32 [8, 2048], P('sx', 'sy'), may hold values from 0 to 511, as said below
Outputs:
- solution: float32 [8, 32, 2048], P('sx', None, 'sy')
- residual: float32 [8, 32, 2048], P('sx', None, 'sy')
Inputs may be any that keep to these rules, and one draw needn't show every extreme that they name: `schur`: each subdomain's matrix is symmetric positive definite. `precond`: each subdomain's matrix is symmetric positive definite. `matching`: each aligned block of 512 entries of a row is a permutation of 0 to 511.
All inputs are finite; a program needn't handle non-finite values.
Results may differ from a plain program's by a relative error of at most 0.007.
The roundings to bfloat16 on the way count: a program that leaves them out, or rounds other values in their place, can miss the bound.
Values may be sent and summed in bfloat16 or wider, within the bound.
No kernel may reach another device: no remote copies, remote signals or barrier semaphores. Data moves between devices by JAX's collectives and lax.ppermute only.
A program may use at most 64 MiB of HBM per device.

v0:
```python
import jax
import jax.numpy as jnp
from jax import lax
from jax.sharding import PartitionSpec as P

ITERS = 2


def passed_along(block, axis, distance):
    devices = range(lax.axis_size(axis))
    route = [((i - distance) % len(devices), i) for i in devices]
    return lax.ppermute(block, axis, route)


def apply_op(matrix, block, match_loc, inverse):
    rows_here = matrix.shape[0]
    half = rows_here // 2
    sent = jnp.take(block, match_loc, axis=1)
    right_part = passed_along(sent, "sx", -1)
    local = jnp.concatenate([block, right_part], axis=1)
    prod = lax.dot_general(
        lax.all_gather(local, "sy", axis=1, tiled=True),
        matrix,
        (((1,), (1,)), ((), ())),
        preferred_element_type=jnp.float32,
    )
    left_out = prod[:, :half]
    right_out = prod[:, half:]
    came = passed_along(right_out, "sx", 1)
    return left_out + jnp.take(came, inverse, axis=1)


def gram(first, second):
    partial_sum = jnp.dot(first, second.T, precision=lax.Precision.HIGHEST)
    total = lax.psum(partial_sum, ("sx", "sy"))
    return 0.5 * (total + total.T)


def solve_spd(matrix, rhs):
    lower = jnp.linalg.cholesky(matrix)
    return jax.scipy.linalg.cho_solve((lower, True), rhs)


def combine(coeff, block):
    return jnp.dot(coeff.T, block, precision=lax.Precision.HIGHEST)


def shards(schur, precond, right_side, matching):
    schur_rows = schur[0]
    precond_rows = precond[0]
    match_loc = matching[0]
    inverse = jnp.argsort(match_loc)
    residual = right_side[0]
    solution = jnp.zeros_like(residual)
    search = apply_op(precond_rows, residual.astype(jnp.bfloat16), match_loc, inverse)
    gamma = gram(residual, search)
    for step in range(ITERS):
        image = apply_op(schur_rows, search.astype(jnp.bfloat16), match_loc, inverse)
        delta = gram(search, image)
        alpha = solve_spd(delta, gamma)
        solution = solution + combine(alpha, search)
        residual = residual - combine(alpha, image)
        if step + 1 < ITERS:
            precd = apply_op(precond_rows, residual.astype(jnp.bfloat16), match_loc, inverse)
            gnew = gram(residual, precd)
            beta = solve_spd(gamma, gnew)
            search = precd + combine(beta, search)
            gamma = gnew
    return (solution[None], residual[None])


def solution(mesh):
    in_specs = (P("sx", "sy", None), P("sx", "sy", None), P("sx", None, "sy"), P("sx", "sy"))
    out_specs = (P("sx", None, "sy"), P("sx", None, "sy"))
    return jax.shard_map(shards, mesh=mesh, in_specs=in_specs, out_specs=out_specs, check_vma=False)
```

profile of v0, /device:TPU:0, one launch (start us, length us, event | category | flops | bytes accessed | tf_op | source)
XLA Modules:
  0.0 250.3 jit_solution(12864554921434175186)
XLA Ops:
  3.0 1.3 gather_fusion
  4.4 6.1 %collective-permute-start = (bf16[32,512]{1,0:T(8,128)(2,1)S(1)}, bf16[32,512]{1,0:T(8,128)(2,1)S(1)}, u32[]{:S(2)}, u32[]{:S(2)}) collective-permute-start(bf16[32,512]{1,0:T(8,128)(2,1)S(1)} %select_bitcast_fusion.3), channel_id=1, source_target_pairs={{4,0},{8,4},{12,8},{16,12},{20,16},{24,20},{28,24},{0,28},{5,1},{9... | collective-permute-start | bytes 98312 | tf_op jit(solution)/shard_map/ppermute | solution.py:12
  10.5 4.4 %sort.17 = (s32[512]{0:T(512)}, s32[512]{0:T(512)S(1)}) sort(s32[512]{0:T(512)} %bitcast.121, s32[512]{0:T(512)S(1)} %iota.35), dimensions={0}, to_apply=%region_0.2 | sort | flops 4608 | bytes 8192 | tf_op jit(solution)/shard_map/jit(argsort)/sort | solution.py:52
  15.0 5.8 %all_gather.12 = bf16[32,4096]{1,0:T(8,128)(2,1)S(1)} all-gather(bf16[32,1024]{1,0:T(8,128)(2,1)S(1)} %pad_maximum_fusion), channel_id=1, replica_groups=mesh['sx'=8,'sy'=4] {'sy'}, dimensions={1}, use_global_device_ids=true | all-gather | bytes 327680 | tf_op jit(solution)/shard_map/all_gather | solution.py:22
  20.8 6.0 %fusion.6 = f32[32,1024]{1,0:T(8,128)S(1)} fusion(bf16[32,4096]{1,0:T(8,128)(2,1)S(1)} %all_gather.12, bf16[1,1024,4096]{2,1,0:T(8,128)(2,1)} %param.12), kind=kOutput, calls=%fused_computation.14 | convolution fusion | flops 268435456 | bytes 8781824 | tf_op jit(solution)/shard_map/dot_general | solution.py:21
  26.9 7.0 %collective-permute-done.1 = f32[32,512]{1,0:T(8,128)S(1)} collective-permute-done((f32[32,512]{1,0:T(8,128)S(1)}, f32[32,512]{1,0:T(8,128)S(1)}, u32[]{:S(2)}, u32[]{:S(2)}) %collective-permute-start.1) | collective-permute-done | bytes 65568 | tf_op jit(solution)/shard_map/ppermute | solution.py:12
  35.3 1.3 gather_fusion.2
  36.8 3.9 %collective-permute-done.2 = bf16[32,512]{1,0:T(8,128)(2,1)S(1)} collective-permute-done((bf16[32,512]{1,0:T(8,128)(2,1)S(1)}, bf16[32,512]{1,0:T(8,128)(2,1)S(1)}, u32[]{:S(2)}, u32[]{:S(2)}) %collective-permute-start.2) | collective-permute-done | bytes 32800 | tf_op jit(solution)/shard_map/ppermute | solution.py:12
  40.7 5.8 %all_gather.13 = bf16[32,4096]{1,0:T(8,128)(2,1)S(1)} all-gather(bf16[32,1024]{1,0:T(8,128)(2,1)S(1)} %pad_maximum_fusion.1), channel_id=1, replica_groups=mesh['sx'=8,'sy'=4] {'sy'}, dimensions={1}, use_global_device_ids=true | all-gather | bytes 327680 | tf_op jit(solution)/shard_map/all_gather | solution.py:22
  46.5 6.0 %fusion.2 = f32[32,1024]{1,0:T(8,128)S(1)} fusion(bf16[32,4096]{1,0:T(8,128)(2,1)S(1)} %all_gather.13, bf16[1,1024,4096]{2,1,0:T(8,128)(2,1)} %param.11), kind=kOutput, calls=%fused_computation.10 | convolution fusion | flops 268435456 | bytes 8781824 | tf_op jit(solution)/shard_map/dot_general | solution.py:21
  52.8 6.8 %collective-permute-done.3 = f32[32,512]{1,0:T(8,128)S(1)} collective-permute-done((f32[32,512]{1,0:T(8,128)S(1)}, f32[32,512]{1,0:T(8,128)S(1)}, u32[]{:S(2)}, u32[]{:S(2)}) %collective-permute-start.3) | collective-permute-done | bytes 65568 | tf_op jit(solution)/shard_map/ppermute | solution.py:12
  61.1 37.1 %all-reduce = (f32[32,32]{1,0:T(8,128)S(1)}, f32[32,32]{1,0:T(8,128)S(1)}) all-reduce(f32[32,32]{1,0:T(8,128)S(1)} %convolution_bitcast_fusion, f32[32,32]{1,0:T(8,128)S(1)} %fusion.11), channel_id=1, replica_groups=mesh['sx'=8,'sy'=4] {'sx','sy'}, use_global_device_ids=true, to_apply=%region_4.8 | all-reduce | flops 2048 | bytes 16384 | tf_op jit(solution)/shard_map/psum | solution.py:35
  98.4 2.9 %cholesky.59 = f32[32,32]{1,0:T(8,128)S(1)} custom-call(f32[32,32]{1,0:T(8,128)S(1)} %fusion.34), custom_call_target="Cholesky" | custom-call | tf_op jit(solution)/shard_map/jit(cholesky)/cholesky | solution.py:40
  102.7 2.4 custom-call.9
  105.8 2.9 %cholesky.70 = f32[32,32]{1,0:T(8,128)S(1)} custom-call(f32[32,32]{1,0:T(8,128)S(1)} %fusion.28), custom_call_target="Cholesky" | custom-call | tf_op jit(solution)/shard_map/jit(cholesky)/cholesky | solution.py:40
  110.4 4.1 %collective-permute-start.4 = (bf16[32,512]{1,0:T(8,128)(2,1)S(1)}, bf16[32,512]{1,0:T(8,128)(2,1)S(1)}, u32[]{:S(2)}, u32[]{:S(2)}) collective-permute-start(bf16[32,512]{1,0:T(8,128)(2,1)S(1)} %select_bitcast_fusion.1), channel_id=1, source_target_pairs={{4,0},{8,4},{12,8},{16,12},{20,16},{24,20},{28,24},{0,28},{5,1},{9... | collective-permute-start | bytes 98312 | tf_op jit(solution)/shard_map/ppermute | solution.py:12
  116.0 5.8 %all_gather.14 = bf16[32,4096]{1,0:T(8,128)(2,1)S(1)} all-gather(bf16[32,1024]{1,0:T(8,128)(2,1)S(1)} %pad_maximum_fusion.2), channel_id=1, replica_groups=mesh['sx'=8,'sy'=4] {'sy'}, dimensions={1}, use_global_device_ids=true | all-gather | bytes 327680 | tf_op jit(solution)/shard_map/all_gather | solution.py:22
  121.8 6.0 %fusion.4 = f32[32,1024]{1,0:T(8,128)S(1)} fusion(bf16[32,4096]{1,0:T(8,128)(2,1)S(1)} %all_gather.14, bf16[1,1024,4096]{2,1,0:T(8,128)(2,1)} %param.12), kind=kOutput, calls=%fused_computation.12 | convolution fusion | flops 268435456 | bytes 8781824 | tf_op jit(solution)/shard_map/dot_general | solution.py:21
  127.8 1.7 collective-permute-start.5
  130.2 2.4 custom-call.10
  132.6 3.0 %collective-permute-done.5 = f32[32,512]{1,0:T(8,128)S(1)} collective-permute-done((f32[32,512]{1,0:T(8,128)S(1)}, f32[32,512]{1,0:T(8,128)S(1)}, u32[]{:S(2)}, u32[]{:S(2)}) %collective-permute-start.5) | collective-permute-done | bytes 65568 | tf_op jit(solution)/shard_map/ppermute | solution.py:12
  137.1 38.3 %psum.30 = f32[32,32]{1,0:T(8,128)S(1)} all-reduce(f32[32,32]{1,0:T(8,128)S(1)} %fusion.12), channel_id=1, replica_groups=mesh['sx'=8,'sy'=4] {'sx','sy'}, use_global_device_ids=true, to_apply=%region_5.10 | all-reduce | flops 1024 | bytes 8192 | tf_op jit(solution)/shard_map/psum | solution.py:35
  176.3 1.3 gather_fusion.6
  177.7 3.4 %collective-permute-start.6 = (bf16[32,512]{1,0:T(8,128)(2,1)S(1)}, bf16[32,512]{1,0:T(8,128)(2,1)S(1)}, u32[]{:S(2)}, u32[]{:S(2)}) collective-permute-start(bf16[32,512]{1,0:T(8,128)(2,1)S(1)} %select_bitcast_fusion), channel_id=1, source_target_pairs={{4,0},{8,4},{12,8},{16,12},{20,16},{24,20},{28,24},{0,28},{5,1},{9... | collective-permute-start | bytes 98312 | tf_op jit(solution)/shard_map/ppermute | solution.py:12
  181.1 1.6 collective-permute-done.6
  182.7 5.8 %all_gather.15 = bf16[32,4096]{1,0:T(8,128)(2,1)S(1)} all-gather(bf16[32,1024]{1,0:T(8,128)(2,1)S(1)} %pad_maximum_fusion.3), channel_id=1, replica_groups=mesh['sx'=8,'sy'=4] {'sy'}, dimensions={1}, use_global_device_ids=true | all-gather | bytes 327680 | tf_op jit(solution)/shard_map/all_gather | solution.py:22
  188.4 6.0 %fusion = f32[32,1024]{1,0:T(8,128)S(1)} fusion(bf16[32,4096]{1,0:T(8,128)(2,1)S(1)} %all_gather.15, bf16[1,1024,4096]{2,1,0:T(8,128)(2,1)} %param.11), kind=kOutput, calls=%fused_computation.8 | convolution fusion | flops 268435456 | bytes 8781824 | tf_op jit(solution)/shard_map/dot_general | solution.py:21
  194.4 2.3 collective-permute-start.7
  196.9 5.1 %collective-permute-done.7 = f32[32,512]{1,0:T(8,128)S(1)} collective-permute-done((f32[32,512]{1,0:T(8,128)S(1)}, f32[32,512]{1,0:T(8,128)S(1)}, u32[]{:S(2)}, u32[]{:S(2)}) %collective-permute-start.7) | collective-permute-done | bytes 65568 | tf_op jit(solution)/shard_map/ppermute | solution.py:12
  203.6 37.7 %psum.31 = f32[32,32]{1,0:T(8,128)S(1)} all-reduce(f32[32,32]{1,0:T(8,128)S(1)} %fusion.13), channel_id=1, replica_groups=mesh['sx'=8,'sy'=4] {'sx','sy'}, use_global_device_ids=true, to_apply=%region_6.11 | all-reduce | flops 1024 | bytes 8192 | tf_op jit(solution)/shard_map/psum | solution.py:35
  241.4 2.9 %cholesky.81 = f32[32,32]{1,0:T(8,128)S(1)} custom-call(f32[32,32]{1,0:T(8,128)S(1)} %fusion.21), custom_call_target="Cholesky" | custom-call | tf_op jit(solution)/shard_map/jit(cholesky)/cholesky | solution.py:40
  245.7 2.4 custom-call.11
  (85 shorter events, 19.7 us)
Async XLA Ops:
  4.4 10.5 %collective-permute-start = (bf16[32,512]{1,0:T(8,128)(2,1)S(1)}, bf16[32,512]{1,0:T(8,128)(2,1)S(1)}, u32[]{:S(2)}, u32[]{:S(2)}) collective-permute-start(bf16[32,512]{1,0:T(8,128)(2,1)S(1)} %select_bitcast_fusion.3), channel_id=1, source_target_pairs={{4,0},{8,4},{12,8},{16,12},{20,16},{24,20},{28,24},{0,28},{5,1},{9... | collective-permute-start | bytes 98312 | tf_op jit(solution)/shard_map/ppermute | solution.py:12
  20.8 31.8 %copy-start = (f32[1,32,512]{2,1,0:T(8,128)S(1)}, f32[1,32,512]{2,1,0:T(8,128)}, u32[]{:S(2)}) copy-start(f32[1,32,512]{2,1,0:T(8,128)} %param.13) | copy-start | bytes 196612
  26.8 7.1 %collective-permute-start.1 = (f32[32,512]{1,0:T(8,128)S(1)}, f32[32,512]{1,0:T(8,128)S(1)}, u32[]{:S(2)}, u32[]{:S(2)}) collective-permute-start(f32[32,512]{1,0:T(8,128)S(1)} %slice.61), channel_id=1, source_target_pairs={{28,0},{0,4},{4,8},{8,12},{12,16},{16,20},{20,24},{24,28},{29,1},{... | collective-permute-start | bytes 196616 | tf_op jit(solution)/shard_map/ppermute | solution.py:12
  36.8 4.0 %collective-permute-start.2 = (bf16[32,512]{1,0:T(8,128)(2,1)S(1)}, bf16[32,512]{1,0:T(8,128)(2,1)S(1)}, u32[]{:S(2)}, u32[]{:S(2)}) collective-permute-start(bf16[32,512]{1,0:T(8,128)(2,1)S(1)} %select_bitcast_fusion.2), channel_id=1, source_target_pairs={{4,0},{8,4},{12,8},{16,12},{20,16},{24,20},{28,24},{0,28},{5,1},{9... | collective-permute-start | bytes 98312 | tf_op jit(solution)/shard_map/ppermute | solution.py:12
  52.5 7.1 %collective-permute-start.3 = (f32[32,512]{1,0:T(8,128)S(1)}, f32[32,512]{1,0:T(8,128)S(1)}, u32[]{:S(2)}, u32[]{:S(2)}) collective-permute-start(f32[32,512]{1,0:T(8,128)S(1)} %slice.63), channel_id=1, source_target_pairs={{28,0},{0,4},{4,8},{8,12},{12,16},{16,20},{20,24},{24,28},{29,1},{... | collective-permute-start | bytes 196616 | tf_op jit(solution)/shard_map/ppermute | solution.py:12
  110.4 5.7 %collective-permute-start.4 = (bf16[32,512]{1,0:T(8,128)(2,1)S(1)}, bf16[32,512]{1,0:T(8,128)(2,1)S(1)}, u32[]{:S(2)}, u32[]{:S(2)}) collective-permute-start(bf16[32,512]{1,0:T(8,128)(2,1)S(1)} %select_bitcast_fusion.1), channel_id=1, source_target_pairs={{4,0},{8,4},{12,8},{16,12},{20,16},{24,20},{28,24},{0,28},{5,1},{9... | collective-permute-start | bytes 98312 | tf_op jit(solution)/shard_map/ppermute | solution.py:12
  127.8 7.8 %collective-permute-start.5 = (f32[32,512]{1,0:T(8,128)S(1)}, f32[32,512]{1,0:T(8,128)S(1)}, u32[]{:S(2)}, u32[]{:S(2)}) collective-permute-start(f32[32,512]{1,0:T(8,128)S(1)} %slice.65), channel_id=1, source_target_pairs={{28,0},{0,4},{4,8},{8,12},{12,16},{16,20},{20,24},{24,28},{29,1},{... | collective-permute-start | bytes 196616 | tf_op jit(solution)/shard_map/ppermute | solution.py:12
  177.7 5.0 %collective-permute-start.6 = (bf16[32,512]{1,0:T(8,128)(2,1)S(1)}, bf16[32,512]{1,0:T(8,128)(2,1)S(1)}, u32[]{:S(2)}, u32[]{:S(2)}) collective-permute-start(bf16[32,512]{1,0:T(8,128)(2,1)S(1)} %select_bitcast_fusion), channel_id=1, source_target_pairs={{4,0},{8,4},{12,8},{16,12},{20,16},{24,20},{28,24},{0,28},{5,1},{9... | collective-permute-start | bytes 98312 | tf_op jit(solution)/shard_map/ppermute | solution.py:12
  194.4 7.7 %collective-permute-start.7 = (f32[32,512]{1,0:T(8,128)S(1)}, f32[32,512]{1,0:T(8,128)S(1)}, u32[]{:S(2)}, u32[]{:S(2)}) collective-permute-start(f32[32,512]{1,0:T(8,128)S(1)} %slice.67), channel_id=1, source_target_pairs={{28,0},{0,4},{4,8},{8,12},{12,16},{16,20},{20,24},{24,28},{29,1},{... | collective-permute-start | bytes 196616 | tf_op jit(solution)/shard_map/ppermute | solution.py:12
where the time goes:
time: 251 us; the launch traced here: 250 us
  blocking collectives  136 us (54%)
  waiting for transfers between devices  28.5 us (11%)
  matrix products  28.4 us (11%)
  other arithmetic  26.8 us (11%)
  starting transfers between devices  17.7 us (7%)
  local copies, waits for them, and re-layouts  11.8 us (5%)
    psum x3, blocking collectives, gram(): total = lax.psum(partial_sum, ('sx', 'sy'))  113 us
    ppermute x8, waiting for transfers between devices, passed_along(): return lax.ppermute(block, axis, route)  28.5 us
    dot_general x4, matrix products, apply_op(): lax.dot_general(lax.all_gather(local, 'sy', axis=1, tiled=True), matrix,...  23.8 us
    all_gather x4, blocking collectives, apply_op(): lax.all_gather(local, 'sy', axis=1, tiled=True)  23.1 us
    ppermute x8, starting transfers between devices, passed_along(): return lax.ppermute(block, axis, route)  17.7 us
    another operation x9, other arithmetic, solve_spd(): lower = jnp.linalg.cholesky(matrix)  10.8 us
    another operation x6, other arithmetic, solve_spd(): return jax.scipy.linalg.cho_solve((lower, True), rhs)  9.26 us
    gather x8, local copies, waits for them, and re-layouts, apply_op(): sent = jnp.take(block, match_loc, axis=1)  5.68 us
  transfers between devices with their start and end apart: 8, of which 7 were waited for; matrix products, arithmetic and copies ran while one was open for 3% of the time, Pallas kernels for 0%

commit v1 on v0

--- a/solution.py
+++ b/solution.py
@@ -2,6 +2,7 @@
 import jax.numpy as jnp
 from jax import lax
 from jax.sharding import PartitionSpec as P
+from jax.lax import all_to_all, axis_size
 
 ITERS = 2
 
@@ -13,16 +14,23 @@
 
 
 def apply_op(matrix, block, match_loc, inverse):
+
+    def bind_slots(s0):
+        next_value = all_to_all(
+            jnp.stack([s0 for _ in range(axis_size("sy"))], 0),
+            axis_name="sy",
+            split_axis=0,
+            concat_axis=0,
+        )
+        return jnp.concatenate(next_value, 1)
+
     rows_here = matrix.shape[0]
     half = rows_here // 2
     sent = jnp.take(block, match_loc, axis=1)
     right_part = passed_along(sent, "sx", -1)
     local = jnp.concatenate([block, right_part], axis=1)
     prod = lax.dot_general(
-        lax.all_gather(local, "sy", axis=1, tiled=True),
-        matrix,
-        (((1,), (1,)), ((), ())),
-        preferred_element_type=jnp.float32,
+        bind_slots(local), matrix, (((1,), (1,)), ((), ())), preferred_element_type=jnp.float32
     )
     left_out = prod[:, :half]
     right_out = prod[:, half:]

time: 251 us -> 262 us (1.044)
  waiting for transfers between devices: 28.5 us -> 39.7 us
  blocking collectives: 136 us -> 129 us
  starting transfers between devices: 17.7 us -> 23.1 us
    all_gather x4 -> x0, blocking collectives: 23.1 us -> none  [apply_op(): lax.all_gather(local, 'sy', axis=1, tiled=True)]
    all_to_all x0 -> x2, blocking collectives: none -> 16.8 us  [bind_slots(): all_to_all(jnp.stack([s0 for _ in range(axis_size('sy'))], 0), axis_name=...]
    all_to_all x0 -> x2, waiting for transfers between devices: none -> 11.3 us  [bind_slots(): all_to_all(jnp.stack([s0 for _ in range(axis_size('sy'))], 0), axis_name=...]
    all_to_all x0 -> x2, starting transfers between devices: none -> 6.81 us  [bind_slots(): all_to_all(jnp.stack([s0 for _ in range(axis_size('sy'))], 0), axis_name=...]
  transfers between devices with their start and end apart: 8 -> 10, of which waited for: 7 -> 8; matrix products, arithmetic and copies ran while one was open for 3% -> 4% of each run, Pallas kernels for 0% -> 0%
where the time goes in v1:
time: 262 us; the launch traced here: 261 us
  blocking collectives  129 us (49%)
  waiting for transfers between devices  39.7 us (15%)
  matrix products  28.3 us (11%)
  other arithmetic  26.8 us (10%)
  starting transfers between devices  23.1 us (9%)
  local copies, waits for them, and re-layouts  13.3 us (5%)
    psum x3, blocking collectives, gram(): total = lax.psum(partial_sum, ('sx', 'sy'))  112 us
    ppermute x8, waiting for transfers between devices, passed_along(): return lax.ppermute(block, axis, route)  28.4 us
    dot_general x4, matrix products, apply_op(): lax.dot_general(bind_slots(local), matrix, (((1,), (1,)), ((), ())), pref...  23.8 us
    all_to_all x2, blocking collectives, bind_slots(): all_to_all(jnp.stack([s0 for _ in range(axis_size('sy'))], 0), axis_name=...  16.8 us
    ppermute x8, starting transfers between devices, passed_along(): return lax.ppermute(block, axis, route)  16.3 us
    all_to_all x2, waiting for transfers between devices, bind_slots(): all_to_all(jnp.stack([s0 for _ in range(axis_size('sy'))], 0), axis_name=...  11.3 us
    another operation x9, other arithmetic, solve_spd(): lower = jnp.linalg.cholesky(matrix)  10.8 us
    another operation x6, other arithmetic, solve_spd(): return jax.scipy.linalg.cho_solve((lower, True), rhs)  9.26 us
  transfers between devices with their start and end apart: 10, of which 8 were waited for; matrix products, arithmetic and copies ran while one was open for 4% of the time, Pallas kernels for 0%

profile of v1, /device:TPU:0, one launch (start us, length us, event | category | flops | bytes accessed | tf_op | source)
XLA Modules:
  0.0 261.0 jit_solution(14725554903969084018)
XLA Ops:
  3.0 1.3 gather_fusion
  4.4 6.1 %collective-permute-start = (bf16[32,512]{1,0:T(8,128)(2,1)S(1)}, bf16[32,512]{1,0:T(8,128)(2,1)S(1)}, u32[]{:S(2)}, u32[]{:S(2)}) collective-permute-start(bf16[32,512]{1,0:T(8,128)(2,1)S(1)} %select_bitcast_fusion.3), channel_id=1, source_target_pairs={{4,0},{8,4},{12,8},{16,12},{20,16},{24,20},{28,24},{0,28},{5,1},{9... | collective-permute-start | bytes 98312 | tf_op jit(solution)/shard_map/ppermute | solution.py:13
  10.5 4.4 %sort.17 = (s32[512]{0:T(512)}, s32[512]{0:T(512)S(1)}) sort(s32[512]{0:T(512)} %bitcast.141, s32[512]{0:T(512)S(1)} %iota.35), dimensions={0}, to_apply=%region_0.2 | sort | flops 4608 | bytes 8192 | tf_op jit(solution)/shard_map/jit(argsort)/sort | solution.py:60
  15.7 3.4 %all-to-all-start = ((bf16[4,32,1024]{2,1,0:T(8,128)(2,1)}), bf16[4,32,1024]{2,1,0:T(8,128)(2,1)S(1)}, u32[]{:S(2)}, u32[]{:S(2)}) async-start(bf16[4,32,1024]{2,1,0:T(8,128)(2,1)} %stack.8), calls=%async_computation | async-start | bytes 524288 | tf_op jit(solution)/shard_map/all_to_all | solution.py:19
  19.1 6.0 %all-to-all-done = bf16[4,32,1024]{2,1,0:T(8,128)(2,1)S(1)} async-done(((bf16[4,32,1024]{2,1,0:T(8,128)(2,1)}), bf16[4,32,1024]{2,1,0:T(8,128)(2,1)S(1)}, u32[]{:S(2)}, u32[]{:S(2)}) %all-to-all-start) | async-done | bytes 262176 | tf_op jit(solution)/shard_map/all_to_all | solution.py:19
  25.1 6.0 %fusion.6 = f32[32,1024]{1,0:T(8,128)S(1)} fusion(bf16[32,4096]{1,0:T(8,128)(2,1)S(1)} %bitcast.131, bf16[1,1024,4096]{2,1,0:T(8,128)(2,1)} %param.12), kind=kOutput, calls=%fused_computation.14 | convolution fusion | flops 268435456 | bytes 8781824 | tf_op jit(solution)/shard_map/dot_general | solution.py:32
  31.2 6.9 %collective-permute-done.1 = f32[32,512]{1,0:T(8,128)S(1)} collective-permute-done((f32[32,512]{1,0:T(8,128)S(1)}, f32[32,512]{1,0:T(8,128)S(1)}, u32[]{:S(2)}, u32[]{:S(2)}) %collective-permute-start.1) | collective-permute-done | bytes 65568 | tf_op jit(solution)/shard_map/ppermute | solution.py:13
  41.1 3.9 %collective-permute-done.2 = bf16[32,512]{1,0:T(8,128)(2,1)S(1)} collective-permute-done((bf16[32,512]{1,0:T(8,128)(2,1)S(1)}, bf16[32,512]{1,0:T(8,128)(2,1)S(1)}, u32[]{:S(2)}, u32[]{:S(2)}) %collective-permute-start.2) | collective-permute-done | bytes 32800 | tf_op jit(solution)/shard_map/ppermute | solution.py:13
  45.0 8.4 %all_to_all.20 = bf16[4,32,1024]{2,1,0:T(8,128)(2,1)S(1)} all-to-all(bf16[4,32,1024]{2,1,0:T(8,128)(2,1)S(1)} %stack.9), channel_id=1, replica_groups=mesh['sx'=8,'sy'=4] {'sy'}, dimensions={0} | all-to-all | bytes 524288 | tf_op jit(solution)/shard_map/all_to_all | solution.py:19
  53.4 6.0 %fusion.2 = f32[32,1024]{1,0:T(8,128)S(1)} fusion(bf16[32,4096]{1,0:T(8,128)(2,1)S(1)} %bitcast.132, bf16[1,1024,4096]{2,1,0:T(8,128)(2,1)} %param.11), kind=kOutput, calls=%fused_computation.10 | convolution fusion | flops 268435456 | bytes 8781824 | tf_op jit(solution)/shard_map/dot_general | solution.py:32
  59.7 6.7 %collective-permute-done.3 = f32[32,512]{1,0:T(8,128)S(1)} collective-permute-done((f32[32,512]{1,0:T(8,128)S(1)}, f32[32,512]{1,0:T(8,128)S(1)}, u32[]{:S(2)}, u32[]{:S(2)}) %collective-permute-start.3) | collective-permute-done | bytes 65568 | tf_op jit(solution)/shard_map/ppermute | solution.py:13
  67.9 37.1 %all-reduce = (f32[32,32]{1,0:T(8,128)S(1)}, f32[32,32]{1,0:T(8,128)S(1)}) all-reduce(f32[32,32]{1,0:T(8,128)S(1)} %convolution_bitcast_fusion, f32[32,32]{1,0:T(8,128)S(1)} %fusion.11), channel_id=1, replica_groups=mesh['sx'=8,'sy'=4] {'sx','sy'}, use_global_device_ids=true, to_apply=%region_4.8 | all-reduce | flops 2048 | bytes 16384 | tf_op jit(solution)/shard_map/psum | solution.py:43
  105.2 2.9 %cholesky.59 = f32[32,32]{1,0:T(8,128)S(1)} custom-call(f32[32,32]{1,0:T(8,128)S(1)} %fusion.34), custom_call_target="Cholesky" | custom-call | tf_op jit(solution)/shard_map/jit(cholesky)/cholesky | solution.py:48
  109.5 2.4 custom-call.9
  112.8 1.3 gather_fusion.4
  114.2 4.1 %collective-permute-start.4 = (bf16[32,512]{1,0:T(8,128)(2,1)S(1)}, bf16[32,512]{1,0:T(8,128)(2,1)S(1)}, u32[]{:S(2)}, u32[]{:S(2)}) collective-permute-start(bf16[32,512]{1,0:T(8,128)(2,1)S(1)} %select_bitcast_fusion.1), channel_id=1, source_target_pairs={{4,0},{8,4},{12,8},{16,12},{20,16},{24,20},{28,24},{0,28},{5,1},{9... | collective-permute-start | bytes 98312 | tf_op jit(solution)/shard_map/ppermute | solution.py:13
  118.3 2.9 %cholesky.70 = f32[32,32]{1,0:T(8,128)S(1)} custom-call(f32[32,32]{1,0:T(8,128)S(1)} %fusion.28), custom_call_target="Cholesky" | custom-call | tf_op jit(solution)/shard_map/jit(cholesky)/cholesky | solution.py:48
  122.0 3.4 %all-to-all-start.2 = ((bf16[4,32,1024]{2,1,0:T(8,128)(2,1)}), bf16[4,32,1024]{2,1,0:T(8,128)(2,1)S(1)}, u32[]{:S(2)}, u32[]{:S(2)}) async-start(bf16[4,32,1024]{2,1,0:T(8,128)(2,1)} %stack.10), calls=%async_computation.2 | async-start | bytes 524288 | tf_op jit(solution)/shard_map/all_to_all | solution.py:19
  126.0 5.3 %all-to-all-done.2 = bf16[4,32,1024]{2,1,0:T(8,128)(2,1)S(1)} async-done(((bf16[4,32,1024]{2,1,0:T(8,128)(2,1)}), bf16[4,32,1024]{2,1,0:T(8,128)(2,1)S(1)}, u32[]{:S(2)}, u32[]{:S(2)}) %all-to-all-start.2) | async-done | bytes 262176 | tf_op jit(solution)/shard_map/all_to_all | solution.py:19
  131.4 6.0 %fusion.4 = f32[32,1024]{1,0:T(8,128)S(1)} fusion(bf16[32,4096]{1,0:T(8,128)(2,1)S(1)} %bitcast.133, bf16[1,1024,4096]{2,1,0:T(8,128)(2,1)} %param.12), kind=kOutput, calls=%fused_computation.12 | convolution fusion | flops 268435456 | bytes 8781824 | tf_op jit(solution)/shard_map/dot_general | solution.py:32
  138.4 2.4 custom-call.10
  140.8 3.7 %collective-permute-done.5 = f32[32,512]{1,0:T(8,128)S(1)} collective-permute-done((f32[32,512]{1,0:T(8,128)S(1)}, f32[32,512]{1,0:T(8,128)S(1)}, u32[]{:S(2)}, u32[]{:S(2)}) %collective-permute-start.5) | collective-permute-done | bytes 65568 | tf_op jit(solution)/shard_map/ppermute | solution.py:13
  146.0 37.2 %psum.30 = f32[32,32]{1,0:T(8,128)S(1)} all-reduce(f32[32,32]{1,0:T(8,128)S(1)} %fusion.12), channel_id=1, replica_groups=mesh['sx'=8,'sy'=4] {'sx','sy'}, use_global_device_ids=true, to_apply=%region_5.10 | all-reduce | flops 1024 | bytes 8192 | tf_op jit(solution)/shard_map/psum | solution.py:43
  185.5 4.1 %collective-permute-start.6 = (bf16[32,512]{1,0:T(8,128)(2,1)S(1)}, bf16[32,512]{1,0:T(8,128)(2,1)S(1)}, u32[]{:S(2)}, u32[]{:S(2)}) collective-permute-start(bf16[32,512]{1,0:T(8,128)(2,1)S(1)} %select_bitcast_fusion), channel_id=1, source_target_pairs={{4,0},{8,4},{12,8},{16,12},{20,16},{24,20},{28,24},{0,28},{5,1},{9... | collective-permute-start | bytes 98312 | tf_op jit(solution)/shard_map/ppermute | solution.py:13
  189.6 1.6 collective-permute-done.6
  191.2 8.4 %all_to_all.21 = bf16[4,32,1024]{2,1,0:T(8,128)(2,1)S(1)} all-to-all(bf16[4,32,1024]{2,1,0:T(8,128)(2,1)S(1)} %stack.11), channel_id=1, replica_groups=mesh['sx'=8,'sy'=4] {'sy'}, dimensions={0} | all-to-all | bytes 524288 | tf_op jit(solution)/shard_map/all_to_all | solution.py:19
  199.6 6.0 %fusion = f32[32,1024]{1,0:T(8,128)S(1)} fusion(bf16[32,4096]{1,0:T(8,128)(2,1)S(1)} %bitcast.134, bf16[1,1024,4096]{2,1,0:T(8,128)(2,1)} %param.11), kind=kOutput, calls=%fused_computation.8 | convolution fusion | flops 268435456 | bytes 8781824 | tf_op jit(solution)/shard_map/dot_general | solution.py:32
  205.6 1.6 collective-permute-start.7
  207.4 5.5 %collective-permute-done.7 = f32[32,512]{1,0:T(8,128)S(1)} collective-permute-done((f32[32,512]{1,0:T(8,128)S(1)}, f32[32,512]{1,0:T(8,128)S(1)}, u32[]{:S(2)}, u32[]{:S(2)}) %collective-permute-start.7) | collective-permute-done | bytes 65568 | tf_op jit(solution)/shard_map/ppermute | solution.py:13
  214.4 37.6 %psum.31 = f32[32,32]{1,0:T(8,128)S(1)} all-reduce(f32[32,32]{1,0:T(8,128)S(1)} %fusion.13), channel_id=1, replica_groups=mesh['sx'=8,'sy'=4] {'sx','sy'}, use_global_device_ids=true, to_apply=%region_6.11 | all-reduce | flops 1024 | bytes 8192 | tf_op jit(solution)/shard_map/psum | solution.py:43
  252.2 2.9 %cholesky.81 = f32[32,32]{1,0:T(8,128)S(1)} custom-call(f32[32,32]{1,0:T(8,128)S(1)} %fusion.21), custom_call_target="Cholesky" | custom-call | tf_op jit(solution)/shard_map/jit(cholesky)/cholesky | solution.py:48
  256.4 2.4 custom-call.11
  (95 shorter events, 22.1 us)
Async XLA Ops:
  4.4 10.5 %collective-permute-start = (bf16[32,512]{1,0:T(8,128)(2,1)S(1)}, bf16[32,512]{1,0:T(8,128)(2,1)S(1)}, u32[]{:S(2)}, u32[]{:S(2)}) collective-permute-start(bf16[32,512]{1,0:T(8,128)(2,1)S(1)} %select_bitcast_fusion.3), channel_id=1, source_target_pairs={{4,0},{8,4},{12,8},{16,12},{20,16},{24,20},{28,24},{0,28},{5,1},{9... | collective-permute-start | bytes 98312 | tf_op jit(solution)/shard_map/ppermute | solution.py:13
  15.7 9.4 %all-to-all-start = ((bf16[4,32,1024]{2,1,0:T(8,128)(2,1)}), bf16[4,32,1024]{2,1,0:T(8,128)(2,1)S(1)}, u32[]{:S(2)}, u32[]{:S(2)}) async-start(bf16[4,32,1024]{2,1,0:T(8,128)(2,1)} %stack.8), calls=%async_computation | async-start | bytes 524288 | tf_op jit(solution)/shard_map/all_to_all | solution.py:19
  31.1 28.4 %copy-start = (f32[1,32,512]{2,1,0:T(8,128)S(1)}, f32[1,32,512]{2,1,0:T(8,128)}, u32[]{:S(2)}) copy-start(f32[1,32,512]{2,1,0:T(8,128)} %param.13) | copy-start | bytes 196612
  31.1 7.0 %collective-permute-start.1 = (f32[32,512]{1,0:T(8,128)S(1)}, f32[32,512]{1,0:T(8,128)S(1)}, u32[]{:S(2)}, u32[]{:S(2)}) collective-permute-start(f32[32,512]{1,0:T(8,128)S(1)} %slice.61), channel_id=1, source_target_pairs={{28,0},{0,4},{4,8},{8,12},{12,16},{16,20},{20,24},{24,28},{29,1},{... | collective-permute-start | bytes 196616 | tf_op jit(solution)/shard_map/ppermute | solution.py:13
  41.0 4.0 %collective-permute-start.2 = (bf16[32,512]{1,0:T(8,128)(2,1)S(1)}, bf16[32,512]{1,0:T(8,128)(2,1)S(1)}, u32[]{:S(2)}, u32[]{:S(2)}) collective-permute-start(bf16[32,512]{1,0:T(8,128)(2,1)S(1)} %select_bitcast_fusion.2), channel_id=1, source_target_pairs={{4,0},{8,4},{12,8},{16,12},{20,16},{24,20},{28,24},{0,28},{5,1},{9... | collective-permute-start | bytes 98312 | tf_op jit(solution)/shard_map/ppermute | solution.py:13
  59.4 7.0 %collective-permute-start.3 = (f32[32,512]{1,0:T(8,128)S(1)}, f32[32,512]{1,0:T(8,128)S(1)}, u32[]{:S(2)}, u32[]{:S(2)}) collective-permute-start(f32[32,512]{1,0:T(8,128)S(1)} %slice.63), channel_id=1, source_target_pairs={{28,0},{0,4},{4,8},{8,12},{12,16},{16,20},{20,24},{24,28},{29,1},{... | collective-permute-start | bytes 196616 | tf_op jit(solution)/shard_map/ppermute | solution.py:13
  114.2 7.0 %collective-permute-start.4 = (bf16[32,512]{1,0:T(8,128)(2,1)S(1)}, bf16[32,512]{1,0:T(8,128)(2,1)S(1)}, u32[]{:S(2)}, u32[]{:S(2)}) collective-permute-start(bf16[32,512]{1,0:T(8,128)(2,1)S(1)} %select_bitcast_fusion.1), channel_id=1, source_target_pairs={{4,0},{8,4},{12,8},{16,12},{20,16},{24,20},{28,24},{0,28},{5,1},{9... | collective-permute-start | bytes 98312 | tf_op jit(solution)/shard_map/ppermute | solution.py:13
  122.0 9.4 %all-to-all-start.2 = ((bf16[4,32,1024]{2,1,0:T(8,128)(2,1)}), bf16[4,32,1024]{2,1,0:T(8,128)(2,1)S(1)}, u32[]{:S(2)}, u32[]{:S(2)}) async-start(bf16[4,32,1024]{2,1,0:T(8,128)(2,1)} %stack.10), calls=%async_computation.2 | async-start | bytes 524288 | tf_op jit(solution)/shard_map/all_to_all | solution.py:19
  137.4 7.2 %collective-permute-start.5 = (f32[32,512]{1,0:T(8,128)S(1)}, f32[32,512]{1,0:T(8,128)S(1)}, u32[]{:S(2)}, u32[]{:S(2)}) collective-permute-start(f32[32,512]{1,0:T(8,128)S(1)} %slice.65), channel_id=1, source_target_pairs={{28,0},{0,4},{4,8},{8,12},{12,16},{16,20},{20,24},{24,28},{29,1},{... | collective-permute-start | bytes 196616 | tf_op jit(solution)/shard_map/ppermute | solution.py:13
  185.5 5.7 %collective-permute-start.6 = (bf16[32,512]{1,0:T(8,128)(2,1)S(1)}, bf16[32,512]{1,0:T(8,128)(2,1)S(1)}, u32[]{:S(2)}, u32[]{:S(2)}) collective-permute-start(bf16[32,512]{1,0:T(8,128)(2,1)S(1)} %select_bitcast_fusion), channel_id=1, source_target_pairs={{4,0},{8,4},{12,8},{16,12},{20,16},{24,20},{28,24},{0,28},{5,1},{9... | collective-permute-start | bytes 98312 | tf_op jit(solution)/shard_map/ppermute | solution.py:13
  205.6 7.3 %collective-permute-start.7 = (f32[32,512]{1,0:T(8,128)S(1)}, f32[32,512]{1,0:T(8,128)S(1)}, u32[]{:S(2)}, u32[]{:S(2)}) collective-permute-start(f32[32,512]{1,0:T(8,128)S(1)} %slice.67), channel_id=1, source_target_pairs={{28,0},{0,4},{4,8},{8,12},{12,16},{16,20},{20,24},{24,28},{29,1},{... | collective-permute-start | bytes 196616 | tf_op jit(solution)/shard_map/ppermute | solution.py:13
